TPU v7x, 1024 devices: a whole 4x8x16 slice. The times are simulated.
1024 devices in a mesh: ctx: 128 (over y, z), head: 8 (over x, core).
Axes of the slice: x: 4, y: 8, z: 16, core: 2. Of those that a mesh axis runs over, the one named last changes fastest.
Arguments:
- queries: bfloat16 [32768, 4096], P('ctx', 'head'), may hold values from -8 to 8
- keys: bfloat16 [32768, 1024], P('ctx', 'head'), may hold values from -6 to 6
- values: bfloat16 [32768, 1024], P('ctx', 'head'), may hold values from -6 to 6
- segment_ids: int32 [32768], P('ctx'), may hold values from 0 to 31, never falling along the last dimension, each value on 1 to 1792 neighbouring positions
- out_weight: bfloat16 [4096, 4096], P('head'), may hold values from -0.125 to 0.125
Outputs:
- mixed: bfloat16 [32768, 4096], P('ctx', 'head')
Inputs may be any that keep to these rules, and one draw needn't show every extreme that they name: `segment_ids`: documents are contiguous runs of tokens; none is longer than 1792 tokens and one is exactly that long.
All inputs are finite; a program needn't handle non-finite values.
Results may differ from a plain program's by a relative error of at most 0.015.
Values may be sent and summed in bfloat16 or wider, within the bound.
A program may use at most 32 MiB of HBM per device.

v0:
```python
import math

import jax
import jax.numpy as jnp
from jax import lax
from jax.sharding import PartitionSpec as P

HEAD_DIM = 128


def shifted(array, axis, by):
    count = lax.axis_size(axis)
    pairs = [(i, i + by) for i in range(count) if 0 <= i + by < count]
    return lax.ppermute(array, axis, pairs)


def body(queries, keys, values, segment_ids, out_weight):
    tokens = queries.shape[0]
    kv_width = keys.shape[1]
    kv_local = kv_width // HEAD_DIM
    repeats = queries.shape[1] // kv_width
    scale = 1.0 / math.sqrt(HEAD_DIM)
    place = lax.axis_index("ctx")
    span = max(lax.axis_size("ctx") // 16, 2)
    grouped = queries.reshape(tokens, kv_local, repeats, HEAD_DIM)
    query_pos = place * tokens + jnp.arange(tokens, dtype=jnp.int32)

    def absorb(carry, packed, key_doc, key_pos):
        count = packed.shape[1]
        visible = (key_pos[None, :] <= query_pos[:, None]) & (key_pos[None, :] >= 0)
        visible = visible & (key_doc[None, :] == segment_ids[:, None])
        top, total, summed = carry
        keyset = packed[0].reshape(count, kv_local, HEAD_DIM)
        valset = packed[1].reshape(count, kv_local, HEAD_DIM)
        scores = (
            jnp.einsum("qgrd,kgd->grqk", grouped, keyset, preferred_element_type=jnp.float32)
            * scale
        )
        fresh = jnp.maximum(top, jnp.max(jnp.where(visible, scores, -1e30), axis=-1))
        weights = jnp.where(visible, jnp.exp(scores - fresh[..., None]), 0.0)
        factor = jnp.exp(top - fresh)
        total = total * factor + jnp.sum(weights, axis=-1)
        update = jnp.einsum(
            "grqk,kgd->grqd",
            weights.astype(jnp.bfloat16),
            valset,
            preferred_element_type=jnp.float32,
        )
        summed = summed * factor[..., None] + update
        return (fresh, total, summed)

    start_top = jnp.full((kv_local, repeats, tokens), -1e30, jnp.float32)
    start_total = jnp.zeros((kv_local, repeats, tokens), jnp.float32)
    start_sum = jnp.zeros((kv_local, repeats, tokens, HEAD_DIM), jnp.float32)
    own_pair = jnp.stack([keys, values], axis=0)
    carry = absorb((start_top, start_total, start_sum), own_pair, segment_ids, query_pos)
    offsets = jnp.arange(tokens, dtype=jnp.int32)

    def turn(step, state):
        inner, pair, docs = state
        pair, docs = shifted((pair, docs), "ctx", 1)
        key_pos = (place - step) * tokens + offsets
        return (absorb(inner, pair, docs, key_pos), pair, docs)

    carry, last_pair, last_docs = lax.fori_loop(1, span, turn, (carry, own_pair, segment_ids))
    final_top, final_total, final_sum = carry
    attended = final_sum / final_total[..., None]
    attended = jnp.transpose(attended, (2, 0, 1, 3)).reshape(tokens, kv_local * repeats * HEAD_DIM)
    attended = attended.astype(jnp.bfloat16)
    partial_out = jnp.dot(attended, out_weight, preferred_element_type=jnp.float32)
    mixed = lax.psum_scatter(
        partial_out.astype(jnp.bfloat16), "head", scatter_dimension=1, tiled=True
    )
    return mixed


def solution(mesh):
    in_specs = (P("ctx", "head"), P("ctx", "head"), P("ctx", "head"), P("ctx"), P("head", None))
    out_specs = P("ctx", "head")
    return jax.shard_map(body, mesh=mesh, in_specs=in_specs, out_specs=out_specs, check_vma=False)
```

profile of v0, /device:TPU:7, one launch (start us, length us, event | category | flops | bytes accessed | tf_op | source)
XLA Modules:
  0.0 164.7 jit_solution(17557370486659338175)
XLA Ops:
  12.4 80.5 %while.22 = (s32[]{:T(128)}, f32[1,4,256]{2,1,0:T(4,128)S(1)}, f32[1,4,256]{2,1,0:T(4,128)S(1)}, f32[1,4,256,128]{3,2,1,0:T(8,128)S(1)}, bf16[2,256,128]{2,1,0:T...) while((s32[]{:T(128)}, f32[1,4,256]{2,1,0:T(4,128)S(1)}, ...), condition=%wide.region_5.6_spmd.clone, body=%wide.region_2.5_spmd.clone.sunk | while | flops 137105408 | bytes 5714665 | solution.py:65
  12.4 4.0 %collective-permute-start = (s32[256]{0:T(256)S(1)}, s32[256]{0:T(256)S(1)}, u32[]{:S(2)}, u32[]{:S(2)}) collective-permute-start(s32[256]{0:T(256)S(1)} %get-tuple-element.347), channel_id=1, source_target_pairs={{0,8},{8,16},{16,24},{24,32},{32,40},{40,48},{48,56},{56,64},{64,7... | collective-permute-start | bytes 3080 | tf_op jit(solution)/shard_map/while/body/eval_jaxpr/ppermute | solution.py:14
  16.4 4.0 %collective-permute-start.1 = (bf16[2,256,128]{2,1,0:T(8,128)(2,1)S(1)}, bf16[2,256,128]{2,1,0:T(8,128)(2,1)S(1)}, u32[]{:S(2)}, u32[]{:S(2)}) collective-permute-start(bf16[2,256,128]{2,1,0:T(8,128)(2,1)S(1)} %get-tuple-element.346), channel_id=1, source_target_pairs={{0,8},{8,16},{16,24},{24,32},{32,40},{40,48},{48,56},{56,64},{64,7... | collective-permute-start | bytes 393224 | tf_op jit(solution)/shard_map/while/body/eval_jaxpr/ppermute | solution.py:14
  20.6 1.7 %collective-permute-done.1 = bf16[2,256,128]{2,1,0:T(8,128)(2,1)S(1)} collective-permute-done((bf16[2,256,128]{2,1,0:T(8,128)(2,1)S(1)}, bf16[2,256,128]{2,1,0:T(8,128)(2,1)S(1)}, u32[]{:S(2)}, u32[]{:S(2)}) %collective-permute-start.1) | collective-permute-done | bytes 131104 | tf_op jit(solution)/shard_map/while/body/eval_jaxpr/ppermute | solution.py:14
  23.4 4.0 %collective-permute-start = (s32[256]{0:T(256)S(1)}, s32[256]{0:T(256)S(1)}, u32[]{:S(2)}, u32[]{:S(2)}) collective-permute-start(s32[256]{0:T(256)S(1)} %get-tuple-element.347), channel_id=1, source_target_pairs={{0,8},{8,16},{16,24},{24,32},{32,40},{40,48},{48,56},{56,64},{64,7... | collective-permute-start | bytes 3080 | tf_op jit(solution)/shard_map/while/body/eval_jaxpr/ppermute | solution.py:14
  27.4 5.2 %collective-permute-start.1 = (bf16[2,256,128]{2,1,0:T(8,128)(2,1)S(1)}, bf16[2,256,128]{2,1,0:T(8,128)(2,1)S(1)}, u32[]{:S(2)}, u32[]{:S(2)}) collective-permute-start(bf16[2,256,128]{2,1,0:T(8,128)(2,1)S(1)} %get-tuple-element.346), channel_id=1, source_target_pairs={{0,8},{8,16},{16,24},{24,32},{32,40},{40,48},{48,56},{56,64},{64,7... | collective-permute-start | bytes 393224 | tf_op jit(solution)/shard_map/while/body/eval_jaxpr/ppermute | solution.py:14
  32.9 1.7 %collective-permute-done.1 = bf16[2,256,128]{2,1,0:T(8,128)(2,1)S(1)} collective-permute-done((bf16[2,256,128]{2,1,0:T(8,128)(2,1)S(1)}, bf16[2,256,128]{2,1,0:T(8,128)(2,1)S(1)}, u32[]{:S(2)}, u32[]{:S(2)}) %collective-permute-start.1) | collective-permute-done | bytes 131104 | tf_op jit(solution)/shard_map/while/body/eval_jaxpr/ppermute | solution.py:14
  35.7 4.0 %collective-permute-start = (s32[256]{0:T(256)S(1)}, s32[256]{0:T(256)S(1)}, u32[]{:S(2)}, u32[]{:S(2)}) collective-permute-start(s32[256]{0:T(256)S(1)} %get-tuple-element.347), channel_id=1, source_target_pairs={{0,8},{8,16},{16,24},{24,32},{32,40},{40,48},{48,56},{56,64},{64,7... | collective-permute-start | bytes 3080 | tf_op jit(solution)/shard_map/while/body/eval_jaxpr/ppermute | solution.py:14
  39.7 5.0 %collective-permute-start.1 = (bf16[2,256,128]{2,1,0:T(8,128)(2,1)S(1)}, bf16[2,256,128]{2,1,0:T(8,128)(2,1)S(1)}, u32[]{:S(2)}, u32[]{:S(2)}) collective-permute-start(bf16[2,256,128]{2,1,0:T(8,128)(2,1)S(1)} %get-tuple-element.346), channel_id=1, source_target_pairs={{0,8},{8,16},{16,24},{24,32},{32,40},{40,48},{48,56},{56,64},{64,7... | collective-permute-start | bytes 393224 | tf_op jit(solution)/shard_map/while/body/eval_jaxpr/ppermute | solution.py:14
  45.0 1.7 %collective-permute-done.1 = bf16[2,256,128]{2,1,0:T(8,128)(2,1)S(1)} collective-permute-done((bf16[2,256,128]{2,1,0:T(8,128)(2,1)S(1)}, bf16[2,256,128]{2,1,0:T(8,128)(2,1)S(1)}, u32[]{:S(2)}, u32[]{:S(2)}) %collective-permute-start.1) | collective-permute-done | bytes 131104 | tf_op jit(solution)/shard_map/while/body/eval_jaxpr/ppermute | solution.py:14
  47.8 3.8 %collective-permute-start = (s32[256]{0:T(256)S(1)}, s32[256]{0:T(256)S(1)}, u32[]{:S(2)}, u32[]{:S(2)}) collective-permute-start(s32[256]{0:T(256)S(1)} %get-tuple-element.347), channel_id=1, source_target_pairs={{0,8},{8,16},{16,24},{24,32},{32,40},{40,48},{48,56},{56,64},{64,7... | collective-permute-start | bytes 3080 | tf_op jit(solution)/shard_map/while/body/eval_jaxpr/ppermute | solution.py:14
  51.6 4.5 %collective-permute-start.1 = (bf16[2,256,128]{2,1,0:T(8,128)(2,1)S(1)}, bf16[2,256,128]{2,1,0:T(8,128)(2,1)S(1)}, u32[]{:S(2)}, u32[]{:S(2)}) collective-permute-start(bf16[2,256,128]{2,1,0:T(8,128)(2,1)S(1)} %get-tuple-element.346), channel_id=1, source_target_pairs={{0,8},{8,16},{16,24},{24,32},{32,40},{40,48},{48,56},{56,64},{64,7... | collective-permute-start | bytes 393224 | tf_op jit(solution)/shard_map/while/body/eval_jaxpr/ppermute | solution.py:14
  56.3 1.7 %collective-permute-done.1 = bf16[2,256,128]{2,1,0:T(8,128)(2,1)S(1)} collective-permute-done((bf16[2,256,128]{2,1,0:T(8,128)(2,1)S(1)}, bf16[2,256,128]{2,1,0:T(8,128)(2,1)S(1)}, u32[]{:S(2)}, u32[]{:S(2)}) %collective-permute-start.1) | collective-permute-done | bytes 131104 | tf_op jit(solution)/shard_map/while/body/eval_jaxpr/ppermute | solution.py:14
  59.1 3.8 %collective-permute-start = (s32[256]{0:T(256)S(1)}, s32[256]{0:T(256)S(1)}, u32[]{:S(2)}, u32[]{:S(2)}) collective-permute-start(s32[256]{0:T(256)S(1)} %get-tuple-element.347), channel_id=1, source_target_pairs={{0,8},{8,16},{16,24},{24,32},{32,40},{40,48},{48,56},{56,64},{64,7... | collective-permute-start | bytes 3080 | tf_op jit(solution)/shard_map/while/body/eval_jaxpr/ppermute | solution.py:14
  62.9 5.0 %collective-permute-start.1 = (bf16[2,256,128]{2,1,0:T(8,128)(2,1)S(1)}, bf16[2,256,128]{2,1,0:T(8,128)(2,1)S(1)}, u32[]{:S(2)}, u32[]{:S(2)}) collective-permute-start(bf16[2,256,128]{2,1,0:T(8,128)(2,1)S(1)} %get-tuple-element.346), channel_id=1, source_target_pairs={{0,8},{8,16},{16,24},{24,32},{32,40},{40,48},{48,56},{56,64},{64,7... | collective-permute-start | bytes 393224 | tf_op jit(solution)/shard_map/while/body/eval_jaxpr/ppermute | solution.py:14
  68.1 1.7 %collective-permute-done.1 = bf16[2,256,128]{2,1,0:T(8,128)(2,1)S(1)} collective-permute-done((bf16[2,256,128]{2,1,0:T(8,128)(2,1)S(1)}, bf16[2,256,128]{2,1,0:T(8,128)(2,1)S(1)}, u32[]{:S(2)}, u32[]{:S(2)}) %collective-permute-start.1) | collective-permute-done | bytes 131104 | tf_op jit(solution)/shard_map/while/body/eval_jaxpr/ppermute | solution.py:14
  70.9 3.9 %collective-permute-start = (s32[256]{0:T(256)S(1)}, s32[256]{0:T(256)S(1)}, u32[]{:S(2)}, u32[]{:S(2)}) collective-permute-start(s32[256]{0:T(256)S(1)} %get-tuple-element.347), channel_id=1, source_target_pairs={{0,8},{8,16},{16,24},{24,32},{32,40},{40,48},{48,56},{56,64},{64,7... | collective-permute-start | bytes 3080 | tf_op jit(solution)/shard_map/while/body/eval_jaxpr/ppermute | solution.py:14
  74.8 4.2 %collective-permute-start.1 = (bf16[2,256,128]{2,1,0:T(8,128)(2,1)S(1)}, bf16[2,256,128]{2,1,0:T(8,128)(2,1)S(1)}, u32[]{:S(2)}, u32[]{:S(2)}) collective-permute-start(bf16[2,256,128]{2,1,0:T(8,128)(2,1)S(1)} %get-tuple-element.346), channel_id=1, source_target_pairs={{0,8},{8,16},{16,24},{24,32},{32,40},{40,48},{48,56},{56,64},{64,7... | collective-permute-start | bytes 393224 | tf_op jit(solution)/shard_map/while/body/eval_jaxpr/ppermute | solution.py:14
  79.2 1.7 %collective-permute-done.1 = bf16[2,256,128]{2,1,0:T(8,128)(2,1)S(1)} collective-permute-done((bf16[2,256,128]{2,1,0:T(8,128)(2,1)S(1)}, bf16[2,256,128]{2,1,0:T(8,128)(2,1)S(1)}, u32[]{:S(2)}, u32[]{:S(2)}) %collective-permute-start.1) | collective-permute-done | bytes 131104 | tf_op jit(solution)/shard_map/while/body/eval_jaxpr/ppermute | solution.py:14
  82.1 3.8 %collective-permute-start = (s32[256]{0:T(256)S(1)}, s32[256]{0:T(256)S(1)}, u32[]{:S(2)}, u32[]{:S(2)}) collective-permute-start(s32[256]{0:T(256)S(1)} %get-tuple-element.347), channel_id=1, source_target_pairs={{0,8},{8,16},{16,24},{24,32},{32,40},{40,48},{48,56},{56,64},{64,7... | collective-permute-start | bytes 3080 | tf_op jit(solution)/shard_map/while/body/eval_jaxpr/ppermute | solution.py:14
  85.8 4.0 %collective-permute-start.1 = (bf16[2,256,128]{2,1,0:T(8,128)(2,1)S(1)}, bf16[2,256,128]{2,1,0:T(8,128)(2,1)S(1)}, u32[]{:S(2)}, u32[]{:S(2)}) collective-permute-start(bf16[2,256,128]{2,1,0:T(8,128)(2,1)S(1)} %get-tuple-element.346), channel_id=1, source_target_pairs={{0,8},{8,16},{16,24},{24,32},{32,40},{40,48},{48,56},{56,64},{64,7... | collective-permute-start | bytes 393224 | tf_op jit(solution)/shard_map/while/body/eval_jaxpr/ppermute | solution.py:14
  90.1 1.7 %collective-permute-done.1 = bf16[2,256,128]{2,1,0:T(8,128)(2,1)S(1)} collective-permute-done((bf16[2,256,128]{2,1,0:T(8,128)(2,1)S(1)}, bf16[2,256,128]{2,1,0:T(8,128)(2,1)S(1)}, u32[]{:S(2)}, u32[]{:S(2)}) %collective-permute-start.1) | collective-permute-done | bytes 131104 | tf_op jit(solution)/shard_map/while/body/eval_jaxpr/ppermute | solution.py:14
  93.2 4.8 %convolution_convert_fusion = bf16[256,4096]{1,0:T(8,128)(2,1)} fusion(bf16[256,512]{0,1:T(8,128)(2,1)S(1)} %bitcast.92, bf16[512,4096]{1,0:T(8,128)(2,1)} %param.11), kind=kOutput, calls=%fused_computation.26 | convolution fusion | flops 1074790400 | bytes 6553600 | tf_op jit(solution)/shard_map/dot_general | solution.py:70
  98.0 59.8 %reduce-scatter.2.cloned.1.call-done = bf16[256,512]{1,0:T(8,128)(2,1)} async-done(((bf16[256,4096]{1,0:T(8,128)(2,1)}), bf16[256,512]{1,0:T(8,128)(2,1)}) %reduce-scatter.2.cloned.1.call-update) | async-done | bytes 262160 | tf_op jit(solution)/shard_map/reduce_scatter | solution.py:71
  (106 shorter events, 14.9 us)
Async XLA Ops:
  6.5 5.8 %copy-start.2 = (s32[256]{0:T(256)S(1)}, s32[256]{0:T(256)}, u32[]{:S(2)}) copy-start(s32[256]{0:T(256)} %param.10) | copy-start | bytes 3076
  6.5 5.8 %copy-start = (bf16[256,128]{1,0:T(8,128)(2,1)S(1)}, bf16[256,128]{1,0:T(8,128)(2,1)}, u32[]{:S(2)}) copy-start(bf16[256,128]{1,0:T(8,128)(2,1)} %param.8) | copy-start | bytes 196612
  6.5 5.8 %copy-start.1 = (bf16[256,128]{1,0:T(8,128)(2,1)S(1)}, bf16[256,128]{1,0:T(8,128)(2,1)}, u32[]{:S(2)}) copy-start(bf16[256,128]{1,0:T(8,128)(2,1)} %param.9) | copy-start | bytes 196612
  6.5 151.3 %reduce-scatter.2.cloned.1.call-start = ((), (), s32[]{:S(2)}) async-start(), calls=%async_computation.1 | async-start | bytes 2359296 | tf_op jit(solution)/shard_map/reduce_scatter | solution.py:71
  12.4 8.1 %collective-permute-start = (s32[256]{0:T(256)S(1)}, s32[256]{0:T(256)S(1)}, u32[]{:S(2)}, u32[]{:S(2)}) collective-permute-start(s32[256]{0:T(256)S(1)} %get-tuple-element.347), channel_id=1, source_target_pairs={{0,8},{8,16},{16,24},{24,32},{32,40},{40,48},{48,56},{56,64},{64,7... | collective-permute-start | bytes 3080 | tf_op jit(solution)/shard_map/while/body/eval_jaxpr/ppermute | solution.py:14
  16.4 5.9 %collective-permute-start.1 = (bf16[2,256,128]{2,1,0:T(8,128)(2,1)S(1)}, bf16[2,256,128]{2,1,0:T(8,128)(2,1)S(1)}, u32[]{:S(2)}, u32[]{:S(2)}) collective-permute-start(bf16[2,256,128]{2,1,0:T(8,128)(2,1)S(1)} %get-tuple-element.346), channel_id=1, source_target_pairs={{0,8},{8,16},{16,24},{24,32},{32,40},{40,48},{48,56},{56,64},{64,7... | collective-permute-start | bytes 393224 | tf_op jit(solution)/shard_map/while/body/eval_jaxpr/ppermute | solution.py:14
  23.4 9.3 %collective-permute-start = (s32[256]{0:T(256)S(1)}, s32[256]{0:T(256)S(1)}, u32[]{:S(2)}, u32[]{:S(2)}) collective-permute-start(s32[256]{0:T(256)S(1)} %get-tuple-element.347), channel_id=1, source_target_pairs={{0,8},{8,16},{16,24},{24,32},{32,40},{40,48},{48,56},{56,64},{64,7... | collective-permute-start | bytes 3080 | tf_op jit(solution)/shard_map/while/body/eval_jaxpr/ppermute | solution.py:14
  27.4 7.2 %collective-permute-start.1 = (bf16[2,256,128]{2,1,0:T(8,128)(2,1)S(1)}, bf16[2,256,128]{2,1,0:T(8,128)(2,1)S(1)}, u32[]{:S(2)}, u32[]{:S(2)}) collective-permute-start(bf16[2,256,128]{2,1,0:T(8,128)(2,1)S(1)} %get-tuple-element.346), channel_id=1, source_target_pairs={{0,8},{8,16},{16,24},{24,32},{32,40},{40,48},{48,56},{56,64},{64,7... | collective-permute-start | bytes 393224 | tf_op jit(solution)/shard_map/while/body/eval_jaxpr/ppermute | solution.py:14
  35.7 9.0 %collective-permute-start = (s32[256]{0:T(256)S(1)}, s32[256]{0:T(256)S(1)}, u32[]{:S(2)}, u32[]{:S(2)}) collective-permute-start(s32[256]{0:T(256)S(1)} %get-tuple-element.347), channel_id=1, source_target_pairs={{0,8},{8,16},{16,24},{24,32},{32,40},{40,48},{48,56},{56,64},{64,7... | collective-permute-start | bytes 3080 | tf_op jit(solution)/shard_map/while/body/eval_jaxpr/ppermute | solution.py:14
  39.7 6.9 %collective-permute-start.1 = (bf16[2,256,128]{2,1,0:T(8,128)(2,1)S(1)}, bf16[2,256,128]{2,1,0:T(8,128)(2,1)S(1)}, u32[]{:S(2)}, u32[]{:S(2)}) collective-permute-start(bf16[2,256,128]{2,1,0:T(8,128)(2,1)S(1)} %get-tuple-element.346), channel_id=1, source_target_pairs={{0,8},{8,16},{16,24},{24,32},{32,40},{40,48},{48,56},{56,64},{64,7... | collective-permute-start | bytes 393224 | tf_op jit(solution)/shard_map/while/body/eval_jaxpr/ppermute | solution.py:14
  47.8 8.3 %collective-permute-start = (s32[256]{0:T(256)S(1)}, s32[256]{0:T(256)S(1)}, u32[]{:S(2)}, u32[]{:S(2)}) collective-permute-start(s32[256]{0:T(256)S(1)} %get-tuple-element.347), channel_id=1, source_target_pairs={{0,8},{8,16},{16,24},{24,32},{32,40},{40,48},{48,56},{56,64},{64,7... | collective-permute-start | bytes 3080 | tf_op jit(solution)/shard_map/while/body/eval_jaxpr/ppermute | solution.py:14
  51.6 6.4 %collective-permute-start.1 = (bf16[2,256,128]{2,1,0:T(8,128)(2,1)S(1)}, bf16[2,256,128]{2,1,0:T(8,128)(2,1)S(1)}, u32[]{:S(2)}, u32[]{:S(2)}) collective-permute-start(bf16[2,256,128]{2,1,0:T(8,128)(2,1)S(1)} %get-tuple-element.346), channel_id=1, source_target_pairs={{0,8},{8,16},{16,24},{24,32},{32,40},{40,48},{48,56},{56,64},{64,7... | collective-permute-start | bytes 393224 | tf_op jit(solution)/shard_map/while/body/eval_jaxpr/ppermute | solution.py:14
  59.1 8.8 %collective-permute-start = (s32[256]{0:T(256)S(1)}, s32[256]{0:T(256)S(1)}, u32[]{:S(2)}, u32[]{:S(2)}) collective-permute-start(s32[256]{0:T(256)S(1)} %get-tuple-element.347), channel_id=1, source_target_pairs={{0,8},{8,16},{16,24},{24,32},{32,40},{40,48},{48,56},{56,64},{64,7... | collective-permute-start | bytes 3080 | tf_op jit(solution)/shard_map/while/body/eval_jaxpr/ppermute | solution.py:14
  62.9 6.9 %collective-permute-start.1 = (bf16[2,256,128]{2,1,0:T(8,128)(2,1)S(1)}, bf16[2,256,128]{2,1,0:T(8,128)(2,1)S(1)}, u32[]{:S(2)}, u32[]{:S(2)}) collective-permute-start(bf16[2,256,128]{2,1,0:T(8,128)(2,1)S(1)} %get-tuple-element.346), channel_id=1, source_target_pairs={{0,8},{8,16},{16,24},{24,32},{32,40},{40,48},{48,56},{56,64},{64,7... | collective-permute-start | bytes 393224 | tf_op jit(solution)/shard_map/while/body/eval_jaxpr/ppermute | solution.py:14
  70.9 8.1 %collective-permute-start = (s32[256]{0:T(256)S(1)}, s32[256]{0:T(256)S(1)}, u32[]{:S(2)}, u32[]{:S(2)}) collective-permute-start(s32[256]{0:T(256)S(1)} %get-tuple-element.347), channel_id=1, source_target_pairs={{0,8},{8,16},{16,24},{24,32},{32,40},{40,48},{48,56},{56,64},{64,7... | collective-permute-start | bytes 3080 | tf_op jit(solution)/shard_map/while/body/eval_jaxpr/ppermute | solution.py:14
  74.8 6.1 %collective-permute-start.1 = (bf16[2,256,128]{2,1,0:T(8,128)(2,1)S(1)}, bf16[2,256,128]{2,1,0:T(8,128)(2,1)S(1)}, u32[]{:S(2)}, u32[]{:S(2)}) collective-permute-start(bf16[2,256,128]{2,1,0:T(8,128)(2,1)S(1)} %get-tuple-element.346), channel_id=1, source_target_pairs={{0,8},{8,16},{16,24},{24,32},{32,40},{40,48},{48,56},{56,64},{64,7... | collective-permute-start | bytes 393224 | tf_op jit(solution)/shard_map/while/body/eval_jaxpr/ppermute | solution.py:14
  82.1 7.9 %collective-permute-start = (s32[256]{0:T(256)S(1)}, s32[256]{0:T(256)S(1)}, u32[]{:S(2)}, u32[]{:S(2)}) collective-permute-start(s32[256]{0:T(256)S(1)} %get-tuple-element.347), channel_id=1, source_target_pairs={{0,8},{8,16},{16,24},{24,32},{32,40},{40,48},{48,56},{56,64},{64,7... | collective-permute-start | bytes 3080 | tf_op jit(solution)/shard_map/while/body/eval_jaxpr/ppermute | solution.py:14
  85.8 6.0 %collective-permute-start.1 = (bf16[2,256,128]{2,1,0:T(8,128)(2,1)S(1)}, bf16[2,256,128]{2,1,0:T(8,128)(2,1)S(1)}, u32[]{:S(2)}, u32[]{:S(2)}) collective-permute-start(bf16[2,256,128]{2,1,0:T(8,128)(2,1)S(1)} %get-tuple-element.346), channel_id=1, source_target_pairs={{0,8},{8,16},{16,24},{24,32},{32,40},{40,48},{48,56},{56,64},{64,7... | collective-permute-start | bytes 393224 | tf_op jit(solution)/shard_map/while/body/eval_jaxpr/ppermute | solution.py:14
Sparse Core Ops, SparseCore 0:
  98.1 59.6 reduce-scatter.1
where the time goes:
time: 165 us
  waiting for transfers between devices  71.7 us (43%)
  starting transfers between devices  59.1 us (36%)
  between operations  13.5 us (8%)
  matrix products  13.2 us (8%)
  other arithmetic  4.16 us (3%)
  local copies, waits for them, and re-layouts  2.3 us (1%)
    reduce_scatter x1, waiting for transfers between devices, body(): lax.psum_scatter(partial_out.astype(jnp.bfloat16), 'head', scatter_dimens...  59.8 us
    ppermute x14, starting transfers between devices, shifted(): return lax.ppermute(array, axis, pairs)  59.1 us
    ppermute x14, waiting for transfers between devices, shifted(): return lax.ppermute(array, axis, pairs)  11.8 us
    dot_general x1, matrix products, body(): jnp.dot(attended, out_weight, preferred_element_type=jnp.float32)  4.82 us
    dot_general x8, matrix products, absorb(): jnp.einsum('grqk,kgd->grqd', weights.astype(jnp.bfloat16), valset, prefer...  4.78 us
    dot_general x8, matrix products, absorb(): jnp.einsum('qgrd,kgd->grqk', grouped, keyset, preferred_element_type=jnp....  3.59 us
  transfers between devices with their start and end apart: 15, of which 8 were waited for; matrix products, arithmetic and copies ran while one was open for 1% of the time, Pallas kernels for 0%

commit v1 on v0

v1 whole, which is shorter than its diff:
```python
import functools
import math

import jax
import jax.numpy as jnp
from jax import lax
from jax.experimental import pallas as pl
from jax.experimental.pallas import tpu as pltpu
from jax.sharding import PartitionSpec as P

HEAD_DIM = 128
DOC_MAX = 1792
MESH = pl.DeviceIdType.MESH
NEG = -1e30
F32 = jnp.float32
BF16 = jnp.bfloat16


def kernel(hops, n_ctx, n_x, q_hbm, k_hbm, v_hbm, s_hbm, w_hbm, o_ref,
           q_own, k_own, v_own, s_own, kbuf, vbuf, sbuf, w_buf, att, acc, top,
           opp, to_p, to_m, relay_p, relay_m, from_m, from_p,
           own_sem, wl_sem, ws_sem, wr_sem, hs_sem, hr_sem, as_sem, ar_sem, xs_sem, xr_sem):
    tokens, width = q_own.shape
    heads = width // HEAD_DIM
    half = tokens // 2
    place = lax.axis_index("ctx")
    head = lax.axis_index("head")
    x, core = head // 2, head % 2
    nxt, prv = lax.rem(place + 1, n_ctx), lax.rem(place + n_ctx - 1, n_ctx)
    partner = (place, x * 2 + (1 - core))
    x_p = (place, lax.rem(x + 1, n_x) * 2 + core)
    x_m = (place, lax.rem(x + n_x - 1, n_x) * 2 + core)
    c = math.log2(math.e) / math.sqrt(HEAD_DIM)

    def remote(src, dst, send, recv, device):
        return pltpu.make_async_remote_copy(
            src_ref=src, dst_ref=dst, send_sem=send, recv_sem=recv,
            device_id=device, device_id_type=MESH)

    local = [pltpu.make_async_copy(src, dst, own_sem.at[i]) for i, (src, dst) in enumerate(
        [(s_hbm, s_own), (k_hbm, k_own), (q_hbm, q_own), (v_hbm, v_own)])]
    for copy in local:
        copy.start()

    barrier = pltpu.get_barrier_semaphore()
    for device in ((nxt, head), (prv, head), partner, x_p, x_m):
        pl.semaphore_signal(barrier, inc=1, device_id=device, device_id_type=MESH)
    pl.semaphore_wait(barrier, 5)

    def own_hop(which):
        src = (s_hbm, k_hbm, v_hbm)[which]
        dst = (sbuf, kbuf, vbuf)[which].at[0]
        return remote(src, dst, hs_sem.at[0, which], hr_sem.at[0, which], (nxt, head))

    def hop(which, step):
        buf = (sbuf, kbuf, vbuf)[which]
        return remote(buf.at[step - 1], buf.at[step], hs_sem.at[step, which],
                      hr_sem.at[step, which], (nxt, head))

    def arrived(which, step):
        buf = (sbuf, kbuf, vbuf)[which]
        return remote(buf.at[step], buf.at[step], hs_sem.at[step, which],
                      hr_sem.at[step, which], (nxt, head))

    for which in range(3):
        own_hop(which).start()

    def w_local(r):
        col = pl.multiple_of((lax.rem(x + r, n_x) * 2 + core) * width, width)
        return pltpu.make_async_copy(
            w_hbm.at[:, pl.ds(col, width)], w_buf.at[r, 0:width, :], wl_sem.at[r])

    def w_remote(r):
        col = pl.multiple_of((lax.rem(x + r, n_x) * 2 + (1 - core)) * width, width)
        return remote(w_hbm.at[:, pl.ds(col, width)], w_buf.at[r, width:2 * width, :],
                      ws_sem.at[r], wr_sem.at[r], partner)

    for r in range(n_x):
        w_local(r).start()
        w_remote(r).start()

    for copy in local:
        copy.wait()

    ones = jnp.ones((tokens, HEAD_DIM), BF16)
    k_iota = lax.broadcasted_iota(jnp.int32, (tokens, tokens), 1)
    q_iota = lax.broadcasted_iota(jnp.int32, (tokens, tokens), 0)
    seg_row = s_own[...].astype(F32)
    first = jnp.min(seg_row, axis=1, keepdims=True)
    count_own = jnp.sum(jnp.where(seg_row == first, 1.0, 0.0), axis=1, keepdims=True).astype(jnp.int32)

    def scores(h, keys):
        return lax.dot_general(q_own[:, h * HEAD_DIM:(h + 1) * HEAD_DIM], keys,
                               (((1,), (1,)), ((), ())), preferred_element_type=F32)

    seg_col = jnp.transpose(jnp.broadcast_to(seg_row, (HEAD_DIM, tokens)))
    seg_col = jnp.concatenate([seg_col] * (tokens // HEAD_DIM), axis=1)
    visible = (seg_col == seg_row) & (k_iota <= q_iota)
    keys = k_own[...]
    v_ext = jnp.concatenate([v_own[...], ones], axis=1)
    for h in range(heads):
        s = jnp.where(visible, scores(h, keys), NEG)
        m = jnp.max(s, axis=1, keepdims=True)
        p = jnp.exp2((s - m) * c)
        acc[h] = jnp.dot(p.astype(BF16), v_ext, preferred_element_type=F32)
        top[h] = jnp.broadcast_to(m, (tokens, HEAD_DIM))

    def absorb(step):
        ids = sbuf[step].astype(F32)
        match = jnp.where(ids == first, 1.0, 0.0)
        count = jnp.sum(match, axis=1, keepdims=True).astype(jnp.int32)
        count = jnp.where(place > step, count, 0)
        visible = (q_iota < count_own) & (k_iota >= tokens - count)
        keys = kbuf[step]
        v_ext = jnp.concatenate([vbuf[step], ones], axis=1)
        for h in range(heads):
            s = jnp.where(visible, scores(h, keys), NEG)
            m_old = top[h][:, 0:1]
            m = jnp.maximum(m_old, jnp.max(s, axis=1, keepdims=True))
            p = jnp.exp2((s - m) * c)
            alpha = jnp.exp2((m_old - m) * c)
            acc[h] = acc[h] * alpha + jnp.dot(p.astype(BF16), v_ext, preferred_element_type=F32)
            top[h] = jnp.broadcast_to(m, (tokens, HEAD_DIM))

    def turn(step, _):
        for which in range(3):
            arrived(which, step - 1).wait_recv()
            hop(which, step).start()
        absorb(step - 1)
        return 0

    lax.fori_loop(1, hops, turn, 0)
    for which in range(3):
        arrived(which, hops - 1).wait_recv()
    absorb(hops - 1)

    def give(h):
        mine = att.at[:, h * HEAD_DIM:(h + 1) * HEAD_DIM]
        theirs = att.at[:, width + h * HEAD_DIM:width + (h + 1) * HEAD_DIM]
        return remote(mine, theirs, as_sem.at[h], ar_sem.at[h], partner)

    for h in range(heads):
        done = acc[h]
        att[:, h * HEAD_DIM:(h + 1) * HEAD_DIM] = (
            done[:, :HEAD_DIM] / done[:, HEAD_DIM:]).astype(BF16)
        give(h).start()

    for r in range(n_x):
        w_local(r).wait()
        w_remote(r).wait()
    for h in range(heads):
        give(h).wait()

    top_rows, low_rows = slice(0, half), slice(half, tokens)

    def project(rows, r):
        return jnp.dot(att[rows, :], w_buf[r], preferred_element_type=F32)

    opp_p = remote(opp.at[top_rows, :], relay_p, xs_sem.at[0], xr_sem.at[0], x_p)
    opp_m = remote(opp.at[low_rows, :], relay_m, xs_sem.at[1], xr_sem.at[1], x_m)
    plain_p = remote(to_p.at[low_rows, :], from_m.at[low_rows, :], xs_sem.at[2], xr_sem.at[2], x_p)
    plain_m = remote(to_m.at[top_rows, :], from_p.at[top_rows, :], xs_sem.at[3], xr_sem.at[3], x_m)
    sum_p = remote(to_p.at[top_rows, :], from_m.at[top_rows, :], xs_sem.at[4], xr_sem.at[4], x_p)
    sum_m = remote(to_m.at[low_rows, :], from_p.at[low_rows, :], xs_sem.at[5], xr_sem.at[5], x_m)

    opp[top_rows, :] = project(top_rows, 2).astype(BF16)
    opp_p.start()
    opp[low_rows, :] = project(low_rows, 2).astype(BF16)
    opp_m.start()
    to_p[low_rows, :] = project(low_rows, 1).astype(BF16)
    plain_p.start()
    to_m[top_rows, :] = project(top_rows, 3).astype(BF16)
    plain_m.start()
    mine_p = project(top_rows, 1)
    opp_p.wait_recv()
    to_p[top_rows, :] = (mine_p + relay_p[...].astype(F32)).astype(BF16)
    sum_p.start()
    mine_m = project(low_rows, 3)
    opp_m.wait_recv()
    to_m[low_rows, :] = (mine_m + relay_m[...].astype(F32)).astype(BF16)
    sum_m.start()
    own_top = project(top_rows, 0)
    own_low = project(low_rows, 0)
    plain_p.wait_recv()
    plain_m.wait_recv()
    sum_p.wait_recv()
    o_ref[top_rows, :] = (own_top + from_m[top_rows, :].astype(F32)
                          + from_p[top_rows, :].astype(F32)).astype(BF16)
    sum_m.wait_recv()
    o_ref[low_rows, :] = (own_low + from_m[low_rows, :].astype(F32)
                          + from_p[low_rows, :].astype(F32)).astype(BF16)
    for copy in (opp_p, opp_m, plain_p, plain_m, sum_p, sum_m):
        copy.wait_send()
    for which in range(3):
        own_hop(which).wait_send()

    def settle(step, _):
        for which in range(3):
            hop(which, step).wait_send()
        return 0

    lax.fori_loop(1, hops, settle, 0)


def solution(mesh):
    n_ctx, n_head = mesh.shape["ctx"], mesh.shape["head"]
    n_x = n_head // 2

    def body(queries, keys, values, segment_ids, out_weight):
        tokens, width = queries.shape
        heads = width // HEAD_DIM
        hops = min(-(-(DOC_MAX - 1) // tokens), n_ctx - 1)
        half = tokens // 2
        any_space = pl.BlockSpec(memory_space=pl.ANY)
        dma = pltpu.SemaphoreType.DMA
        return pl.pallas_call(
            functools.partial(kernel, hops, n_ctx, n_x),
            out_shape=jax.ShapeDtypeStruct((tokens, width), BF16),
            in_specs=[any_space] * 5,
            out_specs=pl.BlockSpec(memory_space=pltpu.VMEM),
            scratch_shapes=[
                pltpu.VMEM((tokens, width), BF16),
                pltpu.VMEM((tokens, HEAD_DIM), BF16),
                pltpu.VMEM((tokens, HEAD_DIM), BF16),
                pltpu.VMEM((1, tokens), jnp.int32),
                pltpu.VMEM((hops, tokens, HEAD_DIM), BF16),
                pltpu.VMEM((hops, tokens, HEAD_DIM), BF16),
                pltpu.VMEM((hops, 1, tokens), jnp.int32),
                pltpu.VMEM((n_x, 2 * width, width), BF16),
                pltpu.VMEM((tokens, 2 * width), BF16),
                pltpu.VMEM((heads, tokens, 2 * HEAD_DIM), F32),
                pltpu.VMEM((heads, tokens, HEAD_DIM), F32),
                pltpu.VMEM((tokens, width), BF16),
                pltpu.VMEM((tokens, width), BF16),
                pltpu.VMEM((tokens, width), BF16),
                pltpu.VMEM((half, width), BF16),
                pltpu.VMEM((half, width), BF16),
                pltpu.VMEM((tokens, width), BF16),
                pltpu.VMEM((tokens, width), BF16),
                dma((4,)),
                dma((n_x,)), dma((n_x,)), dma((n_x,)),
                dma((hops, 3)), dma((hops, 3)),
                dma((heads,)), dma((heads,)),
                dma((6,)), dma((6,)),
            ],
            compiler_params=pltpu.CompilerParams(collective_id=0, has_side_effects=True),
        )(queries, keys, values, segment_ids.reshape(1, tokens), out_weight)

    in_specs = (P("ctx", "head"), P("ctx", "head"), P("ctx", "head"), P("ctx"), P("head", None))
    return jax.shard_map(body, mesh=mesh, in_specs=in_specs, out_specs=P("ctx", "head"), check_vma=False)
```

time: 165 us -> 66 us (0.40)
  the two profiles are of different devices: /device:TPU:7 before, /device:TPU:1 now
where the time goes in v1:
time: 66 us; the launch traced here: 65.8 us
  Pallas kernels  64.1 us (97%)
  local copies, waits for them, and re-layouts  1.67 us (3%)
    pallas_call x1, Pallas kernels, body(): pl.pallas_call(functools.partial(kernel, hops, n_ctx, n_x), out_shape=jax...  64.1 us
    unnamed x1, local copies, waits for them, and re-layouts  1.67 us

profile of v1, /device:TPU:1, one launch (start us, length us, event | category | flops | bytes accessed | tf_op | source)
XLA Modules:
  0.0 65.8 jit_solution(6909203238282202169)
XLA Ops:
  0.0 64.1 %shard_map.55 = bf16[256,512]{1,0:T(8,128)(2,1)} custom-call(bf16[256,512]{1,0:T(8,128)(2,1)} %q_hbm.1, bf16[256,128]{1,0:T(8,128)(2,1)} %k_hbm.1, bf16[256,128]{1,0:T(8,128)(2,1)} %v_hbm.1, s32[1,256]{1,0:T(1,128)} %bitcast.1, bf16[512,4096]{1,0:T(8,128)(2,1)} %w_hbm.1), custom_call_target="tpu_custom_call" | custom-call | tf_op jit(solution)/shard_map/pallas_call | solution.py:216
  64.1 1.7 %copy.7 = bf16[256,512]{1,0:T(8,128)(2,1)} copy(bf16[256,512]{1,0:T(8,128)(2,1)} %shard_map.55) | data formatting | bytes 524288

commit v2 on v1

--- a/solution.py
+++ b/solution.py
@@ -10,6 +10,8 @@
 
 HEAD_DIM = 128
 DOC_MAX = 1792
+RING = 16
+PIECES = 2
 MESH = pl.DeviceIdType.MESH
 NEG = -1e30
 F32 = jnp.float32
@@ -19,7 +21,9 @@
 def kernel(hops, n_ctx, n_x, q_hbm, k_hbm, v_hbm, s_hbm, w_hbm, o_ref,
            q_own, k_own, v_own, s_own, kbuf, vbuf, sbuf, w_buf, att, acc, top,
            opp, to_p, to_m, relay_p, relay_m, from_m, from_p,
-           own_sem, wl_sem, ws_sem, wr_sem, hs_sem, hr_sem, as_sem, ar_sem, xs_sem, xr_sem):
+           via_s, via_k, via_v, wts, fade,
+           own_sem, wl_sem, ws_sem, wr_sem, hs_sem, hr_sem, as_sem, ar_sem, xs_sem, xr_sem,
+           ds_sem, dr_sem, es_sem):
     tokens, width = q_own.shape
     heads = width // HEAD_DIM
     half = tokens // 2
@@ -27,6 +31,13 @@
     head = lax.axis_index("head")
     x, core = head // 2, head % 2
     nxt, prv = lax.rem(place + 1, n_ctx), lax.rem(place + n_ctx - 1, n_ctx)
+    n_row = max(n_ctx // RING, 1)
+    row, col = place // RING, lax.rem(place, RING)
+    detour = hops == 7 and n_ctx % RING == 0 and n_row > 1
+
+    def spot(turns, where):
+        return (lax.rem(row + turns + n_row, n_row) * RING + where, head)
+
     partner = (place, x * 2 + (1 - core))
     x_p = (place, lax.rem(x + 1, n_x) * 2 + core)
     x_m = (place, lax.rem(x + n_x - 1, n_x) * 2 + core)
@@ -43,27 +54,70 @@
         copy.start()
 
     barrier = pltpu.get_barrier_semaphore()
-    for device in ((nxt, head), (prv, head), partner, x_p, x_m):
+
+    def greet(device):
         pl.semaphore_signal(barrier, inc=1, device_id=device, device_id_type=MESH)
-    pl.semaphore_wait(barrier, 5)
+
+    for device in ((prv, head), partner, x_p, x_m):
+        greet(device)
+    if detour:
+        for where, sources in ((5, ((-1, 9),)), (6, ((-1, 10),)), (0, ((0, 5), (0, 1))), (1, ((0, 6),))):
+            @pl.when(col == where)
+            def _():
+                for source in sources:
+                    greet(spot(*source))
+    if detour:
+        further = (col == 9) | (col == 10) | (col == 5) | (col == 6) | (col == 1)
+        pl.semaphore_wait(barrier, jnp.where(further, 5, 4))
+    else:
+        pl.semaphore_wait(barrier, 4)
+
+    piece = tokens // PIECES
+    parts = 1 + 2 * PIECES
+
+    def part(refs, which, *slot):
+        if which == 0:
+            return refs[0].at[slot] if slot else refs[0]
+        at = (which - 1) % PIECES * piece
+        return refs[1 + (which - 1) // PIECES].at[(*slot, slice(at, at + piece), slice(None))]
+
+    given, slots, via = (s_hbm, k_hbm, v_hbm), (sbuf, kbuf, vbuf), (via_s, via_k, via_v)
 
     def own_hop(which):
-        src = (s_hbm, k_hbm, v_hbm)[which]
-        dst = (sbuf, kbuf, vbuf)[which].at[0]
-        return remote(src, dst, hs_sem.at[0, which], hr_sem.at[0, which], (nxt, head))
+        return remote(part(given, which), part(slots, which, 0), hs_sem.at[0, which],
+                      hr_sem.at[0, which], (nxt, head))
 
     def hop(which, step):
-        buf = (sbuf, kbuf, vbuf)[which]
-        return remote(buf.at[step - 1], buf.at[step], hs_sem.at[step, which],
+        return remote(part(slots, which, step - 1), part(slots, which, step), hs_sem.at[step, which],
                       hr_sem.at[step, which], (nxt, head))
 
     def arrived(which, step):
-        buf = (sbuf, kbuf, vbuf)[which]
-        return remote(buf.at[step], buf.at[step], hs_sem.at[step, which],
+        return remote(part(slots, which, step), part(slots, which, step), hs_sem.at[step, which],
                       hr_sem.at[step, which], (nxt, head))
 
-    for which in range(3):
-        own_hop(which).start()
+    def leave(which, where):
+        return remote(part(given, which), part(via, which), ds_sem.at[which], dr_sem.at[which],
+                      spot(1, where))
+
+    def pass_on(which, where):
+        return remote(part(via, which), part(slots, which, 6), es_sem.at[which], hr_sem.at[6, which],
+                      spot(0, where))
+
+    def pass_last(which):
+        return remote(part(slots, which, 6), part(slots, which, 5), es_sem.at[which],
+                      hr_sem.at[5, which], spot(0, 0))
+
+    @pl.when(place < n_ctx - 1)
+    def _():
+        for which in range(parts):
+            own_hop(which).start()
+
+    if detour:
+        for here, where in ((9, 5), (10, 6)):
+            @pl.when((col == here) & (row < n_row - 1))
+            def _():
+                for which in range(parts):
+                    leave(which, where).start()
 
     def w_local(r):
         col = pl.multiple_of((lax.rem(x + r, n_x) * 2 + core) * width, width)
@@ -92,6 +146,14 @@
     def scores(h, keys):
         return lax.dot_general(q_own[:, h * HEAD_DIM:(h + 1) * HEAD_DIM], keys,
                                (((1,), (1,)), ((), ())), preferred_element_type=F32)
+
+    def blank(step, _):
+        kbuf[step] = jnp.zeros((tokens, HEAD_DIM), BF16)
+        vbuf[step] = jnp.zeros((tokens, HEAD_DIM), BF16)
+        sbuf[step] = jnp.full((1, tokens), -1, jnp.int32)
+        return 0
+
+    lax.fori_loop(jnp.minimum(place, hops), hops, blank, 0)
 
     seg_col = jnp.transpose(jnp.broadcast_to(seg_row, (HEAD_DIM, tokens)))
     seg_col = jnp.concatenate([seg_col] * (tokens // HEAD_DIM), axis=1)
@@ -105,45 +167,108 @@
         acc[h] = jnp.dot(p.astype(BF16), v_ext, preferred_element_type=F32)
         top[h] = jnp.broadcast_to(m, (tokens, HEAD_DIM))
 
-    def absorb(step):
+    def weigh(step, which_heads):
         ids = sbuf[step].astype(F32)
-        match = jnp.where(ids == first, 1.0, 0.0)
-        count = jnp.sum(match, axis=1, keepdims=True).astype(jnp.int32)
+        count = jnp.sum(jnp.where(ids == first, 1.0, 0.0), axis=1, keepdims=True).astype(jnp.int32)
         count = jnp.where(place > step, count, 0)
-        visible = (q_iota < count_own) & (k_iota >= tokens - count)
+        start = jnp.where(q_iota[:, 0:1] < count_own, tokens - count, tokens)
         keys = kbuf[step]
-        v_ext = jnp.concatenate([vbuf[step], ones], axis=1)
-        for h in range(heads):
-            s = jnp.where(visible, scores(h, keys), NEG)
+        for h in which_heads:
+            s = jnp.where(k_iota >= start, scores(h, keys), NEG)
             m_old = top[h][:, 0:1]
             m = jnp.maximum(m_old, jnp.max(s, axis=1, keepdims=True))
-            p = jnp.exp2((s - m) * c)
-            alpha = jnp.exp2((m_old - m) * c)
-            acc[h] = acc[h] * alpha + jnp.dot(p.astype(BF16), v_ext, preferred_element_type=F32)
+            wts[h] = jnp.exp2((s - m) * c).astype(BF16)
+            fade[h] = jnp.broadcast_to(jnp.exp2((m_old - m) * c), (tokens, HEAD_DIM))
             top[h] = jnp.broadcast_to(m, (tokens, HEAD_DIM))
 
-    def turn(step, _):
-        for which in range(3):
-            arrived(which, step - 1).wait_recv()
-            hop(which, step).start()
-        absorb(step - 1)
+    def gather(step, h):
+        v_ext = jnp.concatenate([vbuf[step], ones], axis=1)
+        return acc[h] * fade[h][:, 0:1] + jnp.dot(wts[h], v_ext, preferred_element_type=F32)
+
+    def gather_all(step, which_heads):
+        for h in which_heads:
+            acc[h] = gather(step, h)
+
+    def onward(step):
+        going = (place >= step) & (place < n_ctx - 1)
+        if detour:
+            going &= jnp.logical_not(((col == RING - 1) & (step >= 5)) | ((col == 0) & (step == 6)))
+        return going
+
+    lower, upper = range(heads // 2), range(heads // 2, heads)
+
+    def turn(step, after):
+        for which in range(parts):
+            @pl.when(place >= step)
+            def _():
+                arrived(which, step - 1).wait_recv()
+
+            @pl.when(onward(step))
+            def _():
+                hop(which, step).start()
+            after(which)
+        if detour:
+            for here, where in ((5, 0), (6, 1)):
+                @pl.when((step == 4) & (col == here) & (row > 0))
+                def _():
+                    for which in range(parts):
+                        leave(which, where).wait_recv()
+                        pass_on(which, where).start()
+
+            @pl.when((step == 4) & (col == 1) & (row > 0))
+            def _():
+                for which in range(parts):
+                    arrived(which, 6).wait_recv()
+                    pass_last(which).start()
+
+    def first_turn(which):
+        if which == PIECES + 1:
+            weigh(0, lower)
+        if which == parts - 1:
+            weigh(0, upper)
+
+    turn(1, first_turn)
+
+    def later(step, _):
+        def after(which):
+            if which == 1:
+                gather_all(step - 2, lower)
+            if which == PIECES:
+                gather_all(step - 2, upper)
+            if which == PIECES + 1:
+                weigh(step - 1, lower)
+            if which == parts - 1:
+                weigh(step - 1, upper)
+
+        turn(step, after)
         return 0
 
-    lax.fori_loop(1, hops, turn, 0)
-    for which in range(3):
-        arrived(which, hops - 1).wait_recv()
-    absorb(hops - 1)
+    lax.fori_loop(2, hops, later, 0)
+    waits = place >= hops
+    if detour:
+        waits &= col != 1
+    if hops > 1:
+        gather_all(hops - 2, range(heads))
+    for wanted in (range(0, PIECES + 1), range(PIECES + 1, parts)):
+        @pl.when(waits)
+        def _():
+            for which in wanted:
+                arrived(which, hops - 1).wait_recv()
+        if 0 in wanted and hops > 1:
+            weigh(hops - 1, range(heads))
 
     def give(h):
         mine = att.at[:, h * HEAD_DIM:(h + 1) * HEAD_DIM]
         theirs = att.at[:, width + h * HEAD_DIM:width + (h + 1) * HEAD_DIM]
         return remote(mine, theirs, as_sem.at[h], ar_sem.at[h], partner)
 
-    for h in range(heads):
-        done = acc[h]
+    def finish(h, done):
         att[:, h * HEAD_DIM:(h + 1) * HEAD_DIM] = (
             done[:, :HEAD_DIM] / done[:, HEAD_DIM:]).astype(BF16)
         give(h).start()
+
+    for h in range(heads):
+        finish(h, gather(hops - 1, h))
 
     for r in range(n_x):
         w_local(r).wait()
@@ -191,15 +316,29 @@
                           + from_p[low_rows, :].astype(F32)).astype(BF16)
     for copy in (opp_p, opp_m, plain_p, plain_m, sum_p, sum_m):
         copy.wait_send()
-    for which in range(3):
-        own_hop(which).wait_send()
+    @pl.when(place < n_ctx - 1)
+    def _():
+        for which in range(parts):
+            own_hop(which).wait_send()
 
     def settle(step, _):
-        for which in range(3):
-            hop(which, step).wait_send()
+        @pl.when(onward(step))
+        def _():
+            for which in range(parts):
+                hop(which, step).wait_send()
         return 0
 
     lax.fori_loop(1, hops, settle, 0)
+    if detour:
+        @pl.when(((col == 9) | (col == 10)) & (row < n_row - 1))
+        def _():
+            for which in range(parts):
+                leave(which, 5).wait_send()
+
+        @pl.when(((col == 5) | (col == 6) | (col == 1)) & (row > 0))
+        def _():
+            for which in range(parts):
+                pass_last(which).wait_send()
 
 
 def solution(mesh):
@@ -211,6 +350,7 @@
         heads = width // HEAD_DIM
         hops = min(-(-(DOC_MAX - 1) // tokens), n_ctx - 1)
         half = tokens // 2
+        parts = 1 + 2 * PIECES
         any_space = pl.BlockSpec(memory_space=pl.ANY)
         dma = pltpu.SemaphoreType.DMA
         return pl.pallas_call(
@@ -237,11 +377,17 @@
                 pltpu.VMEM((half, width), BF16),
                 pltpu.VMEM((tokens, width), BF16),
                 pltpu.VMEM((tokens, width), BF16),
+                pltpu.VMEM((1, tokens), jnp.int32),
+                pltpu.VMEM((tokens, HEAD_DIM), BF16),
+                pltpu.VMEM((tokens, HEAD_DIM), BF16),
+                pltpu.VMEM((heads, tokens, tokens), BF16),
+                pltpu.VMEM((heads, tokens, HEAD_DIM), F32),
                 dma((4,)),
                 dma((n_x,)), dma((n_x,)), dma((n_x,)),
-                dma((hops, 3)), dma((hops, 3)),
+                dma((hops, parts)), dma((hops, parts)),
                 dma((heads,)), dma((heads,)),
                 dma((6,)), dma((6,)),
+                dma((parts,)), dma((parts,)), dma((parts,)),
             ],
             compiler_params=pltpu.CompilerParams(collective_id=0, has_side_effects=True),
         )(queries, keys, values, segment_ids.reshape(1, tokens), out_weight)

time: 66 us -> 58.1 us (0.88)
  the two profiles are of different devices: /device:TPU:1 before, /device:TPU:120 now
where the time goes in v2:
time: 58.1 us; the launch traced here: 57.9 us
  Pallas kernels  56.2 us (97%)
  local copies, waits for them, and re-layouts  1.67 us (3%)
    pallas_call x1, Pallas kernels, body(): pl.pallas_call(functools.partial(kernel, hops, n_ctx, n_x), out_shape=jax...  56.2 us
    unnamed x1, local copies, waits for them, and re-layouts  1.67 us

profile of v2, /device:TPU:120, one launch (start us, length us, event | category | flops | bytes accessed | tf_op | source)
XLA Modules:
  0.0 57.9 jit_solution(2734553060024123000)
XLA Ops:
  0.0 56.2 %shard_map.55 = bf16[256,512]{1,0:T(8,128)(2,1)} custom-call(bf16[256,512]{1,0:T(8,128)(2,1)} %q_hbm.1, bf16[256,128]{1,0:T(8,128)(2,1)} %k_hbm.1, bf16[256,128]{1,0:T(8,128)(2,1)} %v_hbm.1, s32[1,256]{1,0:T(1,128)} %bitcast.1, bf16[512,4096]{1,0:T(8,128)(2,1)} %w_hbm.1), custom_call_target="tpu_custom_call" | custom-call | tf_op jit(solution)/shard_map/pallas_call | solution.py:356
  56.2 1.7 %copy.7 = bf16[256,512]{1,0:T(8,128)(2,1)} copy(bf16[256,512]{1,0:T(8,128)(2,1)} %shard_map.55) | data formatting | bytes 524288

commit v3 on v2

--- a/solution.py
+++ b/solution.py
@@ -18,9 +18,9 @@
 BF16 = jnp.bfloat16
 
 
-def kernel(hops, n_ctx, n_x, q_hbm, k_hbm, v_hbm, s_hbm, w_hbm, o_ref,
+def kernel(hops, n_ctx, n_x, q_hbm, k_hbm, v_hbm, s_hbm, w_hbm, o_ref, from_m, from_p,
            q_own, k_own, v_own, s_own, kbuf, vbuf, sbuf, w_buf, att, acc, top,
-           opp, to_p, to_m, relay_p, relay_m, from_m, from_p,
+           opp, to_p, to_m, relay_p, relay_m, own_sum,
            via_s, via_k, via_v, wts, fade,
            own_sem, wl_sem, ws_sem, wr_sem, hs_sem, hr_sem, as_sem, ar_sem, xs_sem, xr_sem,
            ds_sem, dr_sem, es_sem):
@@ -304,16 +304,15 @@
     opp_m.wait_recv()
     to_m[low_rows, :] = (mine_m + relay_m[...].astype(F32)).astype(BF16)
     sum_m.start()
-    own_top = project(top_rows, 0)
-    own_low = project(low_rows, 0)
+    own_out = pltpu.make_async_copy(own_sum, o_ref, own_sem.at[0])
+    own_sum[top_rows, :] = project(top_rows, 0)
+    own_sum[low_rows, :] = project(low_rows, 0)
+    own_out.start()
     plain_p.wait_recv()
     plain_m.wait_recv()
     sum_p.wait_recv()
-    o_ref[top_rows, :] = (own_top + from_m[top_rows, :].astype(F32)
-                          + from_p[top_rows, :].astype(F32)).astype(BF16)
     sum_m.wait_recv()
-    o_ref[low_rows, :] = (own_low + from_m[low_rows, :].astype(F32)
-                          + from_p[low_rows, :].astype(F32)).astype(BF16)
+    own_out.wait()
     for copy in (opp_p, opp_m, plain_p, plain_m, sum_p, sum_m):
         copy.wait_send()
     @pl.when(place < n_ctx - 1)
@@ -353,11 +352,11 @@
         parts = 1 + 2 * PIECES
         any_space = pl.BlockSpec(memory_space=pl.ANY)
         dma = pltpu.SemaphoreType.DMA
-        return pl.pallas_call(
+        own, from_m, from_p = pl.pallas_call(
             functools.partial(kernel, hops, n_ctx, n_x),
-            out_shape=jax.ShapeDtypeStruct((tokens, width), BF16),
+            out_shape=[jax.ShapeDtypeStruct((tokens, width), kind) for kind in (F32, BF16, BF16)],
             in_specs=[any_space] * 5,
-            out_specs=pl.BlockSpec(memory_space=pltpu.VMEM),
+            out_specs=[any_space] * 3,
             scratch_shapes=[
                 pltpu.VMEM((tokens, width), BF16),
                 pltpu.VMEM((tokens, HEAD_DIM), BF16),
@@ -375,8 +374,7 @@
                 pltpu.VMEM((tokens, width), BF16),
                 pltpu.VMEM((half, width), BF16),
                 pltpu.VMEM((half, width), BF16),
-                pltpu.VMEM((tokens, width), BF16),
-                pltpu.VMEM((tokens, width), BF16),
+                pltpu.VMEM((tokens, width), F32),
                 pltpu.VMEM((1, tokens), jnp.int32),
                 pltpu.VMEM((tokens, HEAD_DIM), BF16),
                 pltpu.VMEM((tokens, HEAD_DIM), BF16),
@@ -391,6 +389,7 @@
             ],
             compiler_params=pltpu.CompilerParams(collective_id=0, has_side_effects=True),
         )(queries, keys, values, segment_ids.reshape(1, tokens), out_weight)
+        return (own + from_m.astype(F32) + from_p.astype(F32)).astype(BF16)
 
     in_specs = (P("ctx", "head"), P("ctx", "head"), P("ctx", "head"), P("ctx"), P("head", None))
     return jax.shard_map(body, mesh=mesh, in_specs=in_specs, out_specs=P("ctx", "head"), check_vma=False)

time: 58.1 us -> 57.2 us (0.985)
  the two profiles are of different devices: /device:TPU:120 before, /device:TPU:48 now
where the time goes in v3:
time: 57.2 us; the launch traced here: 57 us
  Pallas kernels  55 us (96%)
  other arithmetic  1.99 us (3%)
    pallas_call x1, Pallas kernels, body(): pl.pallas_call(functools.partial(kernel, hops, n_ctx, n_x), out_shape=[ja...  55 us
    convert_element_type x1, other arithmetic, body(): return (own + from_m.astype(F32) + from_p.astype(F32)).astype(BF16)  1.99 us

profile of v3, /device:TPU:48, one launch (start us, length us, event | category | flops | bytes accessed | tf_op | source)
XLA Modules:
  0.0 57.0 jit_solution(3990962606103326831)
XLA Ops:
  0.0 55.0 %shard_map.55 = (f32[256,512]{1,0:T(8,128)}, bf16[256,512]{1,0:T(8,128)(2,1)}, bf16[256,512]{1,0:T(8,128)(2,1)}) custom-call(bf16[256,512]{1,0:T(8,128)(2,1)} %q_hbm.1, bf16[256,128]{1,0:T(8,128)(2,1)} %k_hbm.1, bf16[256,128]{1,0:T(8,128)(2,1)} %v_hbm.1, s32[1,256]{1,0:T(1,128)} %bitcast.1, bf16[512,4096]{1,0:T(8,128)(2,1)} %w_hbm.1), custom_call_target="tpu_custom_call" | custom-call | tf_op jit(solution)/shard_map/pallas_call | solution.py:355
  55.0 2.0 %add_convert_fusion = bf16[256,512]{1,0:T(8,128)(2,1)} fusion(bf16[256,512]{1,0:T(8,128)(2,1)} %get-tuple-element.10, f32[256,512]{1,0:T(8,128)} %get-tuple-element.8, bf16[256,512]{1,0:T(8,128)(2,1)} %get-tuple-element.9), kind=kLoop, calls=%fused_computation | loop fusion | flops 655360 | bytes 1310720 | tf_op jit(solution)/shard_map/convert_element_type | solution.py:392

commit v4 on v3

--- a/solution.py
+++ b/solution.py
@@ -11,16 +11,16 @@
 HEAD_DIM = 128
 DOC_MAX = 1792
 RING = 16
-PIECES = 2
+PIECES = 4
 MESH = pl.DeviceIdType.MESH
 NEG = -1e30
 F32 = jnp.float32
 BF16 = jnp.bfloat16
 
 
-def kernel(hops, n_ctx, n_x, q_hbm, k_hbm, v_hbm, s_hbm, w_hbm, o_ref, from_m, from_p,
+def kernel(hops, n_ctx, n_x, q_hbm, k_hbm, v_hbm, s_hbm, w_hbm, o_ref, late,
            q_own, k_own, v_own, s_own, kbuf, vbuf, sbuf, w_buf, att, acc, top,
-           opp, to_p, to_m, relay_p, relay_m, own_sum,
+           opp, to_p, to_m, relay_p, relay_m, early_p, early_m, own_sum,
            via_s, via_k, via_v, wts, fade,
            own_sem, wl_sem, ws_sem, wr_sem, hs_sem, hr_sem, as_sem, ar_sem, xs_sem, xr_sem,
            ds_sem, dr_sem, es_sem):
@@ -190,22 +190,34 @@
             acc[h] = gather(step, h)
 
     def onward(step):
-        going = (place >= step) & (place < n_ctx - 1)
+        going = (place >= step) & (place < n_ctx - 1) & (step < hops)
         if detour:
             going &= jnp.logical_not(((col == RING - 1) & (step >= 5)) | ((col == 0) & (step == 6)))
         return going
 
     lower, upper = range(heads // 2), range(heads // 2, heads)
 
+    def order(turns):
+        if not detour:
+            return turns
+        return jnp.where((col == 0) & (turns >= 4), jnp.where(turns == 4, 6, turns - 1), turns)
+
+    def due(slot):
+        here = place > slot
+        if detour:
+            here &= jnp.logical_not((col == 1) & (slot == 6))
+        return here
+
     def turn(step, after):
+        slot = order(step - 1)
         for which in range(parts):
-            @pl.when(place >= step)
+            @pl.when(due(slot))
             def _():
-                arrived(which, step - 1).wait_recv()
-
-            @pl.when(onward(step))
+                arrived(which, slot).wait_recv()
+
+            @pl.when(onward(slot + 1))
             def _():
-                hop(which, step).start()
+                hop(which, slot + 1).start()
             after(which)
         if detour:
             for here, where in ((5, 0), (6, 1)):
@@ -232,30 +244,28 @@
     def later(step, _):
         def after(which):
             if which == 1:
-                gather_all(step - 2, lower)
+                gather_all(order(step - 2), lower)
             if which == PIECES:
-                gather_all(step - 2, upper)
+                gather_all(order(step - 2), upper)
             if which == PIECES + 1:
-                weigh(step - 1, lower)
+                weigh(order(step - 1), lower)
             if which == parts - 1:
-                weigh(step - 1, upper)
+                weigh(order(step - 1), upper)
 
         turn(step, after)
         return 0
 
     lax.fori_loop(2, hops, later, 0)
-    waits = place >= hops
-    if detour:
-        waits &= col != 1
     if hops > 1:
-        gather_all(hops - 2, range(heads))
+        gather_all(order(hops - 2), range(heads))
+    end = order(hops - 1)
     for wanted in (range(0, PIECES + 1), range(PIECES + 1, parts)):
-        @pl.when(waits)
+        @pl.when(due(end))
         def _():
             for which in wanted:
-                arrived(which, hops - 1).wait_recv()
+                arrived(which, end).wait_recv()
         if 0 in wanted and hops > 1:
-            weigh(hops - 1, range(heads))
+            weigh(end, range(heads))
 
     def give(h):
         mine = att.at[:, h * HEAD_DIM:(h + 1) * HEAD_DIM]
@@ -268,29 +278,35 @@
         give(h).start()
 
     for h in range(heads):
-        finish(h, gather(hops - 1, h))
+        finish(h, gather(end, h))
 
     for r in range(n_x):
         w_local(r).wait()
         w_remote(r).wait()
+
+    top_rows, low_rows = slice(0, half), slice(half, tokens)
+
+    def share(rows, r, side):
+        at = slice(side * width, (side + 1) * width)
+        return jnp.dot(att[rows, at], w_buf[r, at, :], preferred_element_type=F32)
+
+    opp_top, opp_low = share(top_rows, 2, 0), share(low_rows, 2, 0)
     for h in range(heads):
         give(h).wait()
 
-    top_rows, low_rows = slice(0, half), slice(half, tokens)
-
     def project(rows, r):
         return jnp.dot(att[rows, :], w_buf[r], preferred_element_type=F32)
 
     opp_p = remote(opp.at[top_rows, :], relay_p, xs_sem.at[0], xr_sem.at[0], x_p)
     opp_m = remote(opp.at[low_rows, :], relay_m, xs_sem.at[1], xr_sem.at[1], x_m)
-    plain_p = remote(to_p.at[low_rows, :], from_m.at[low_rows, :], xs_sem.at[2], xr_sem.at[2], x_p)
-    plain_m = remote(to_m.at[top_rows, :], from_p.at[top_rows, :], xs_sem.at[3], xr_sem.at[3], x_m)
-    sum_p = remote(to_p.at[top_rows, :], from_m.at[top_rows, :], xs_sem.at[4], xr_sem.at[4], x_p)
-    sum_m = remote(to_m.at[low_rows, :], from_p.at[low_rows, :], xs_sem.at[5], xr_sem.at[5], x_m)
-
-    opp[top_rows, :] = project(top_rows, 2).astype(BF16)
+    plain_p = remote(to_p.at[low_rows, :], early_m, xs_sem.at[2], xr_sem.at[2], x_p)
+    plain_m = remote(to_m.at[top_rows, :], early_p, xs_sem.at[3], xr_sem.at[3], x_m)
+    sum_p = remote(to_p.at[top_rows, :], late.at[top_rows, :], xs_sem.at[4], xr_sem.at[4], x_p)
+    sum_m = remote(to_m.at[low_rows, :], late.at[low_rows, :], xs_sem.at[5], xr_sem.at[5], x_m)
+
+    opp[top_rows, :] = (opp_top + share(top_rows, 2, 1)).astype(BF16)
     opp_p.start()
-    opp[low_rows, :] = project(low_rows, 2).astype(BF16)
+    opp[low_rows, :] = (opp_low + share(low_rows, 2, 1)).astype(BF16)
     opp_m.start()
     to_p[low_rows, :] = project(low_rows, 1).astype(BF16)
     plain_p.start()
@@ -305,14 +321,16 @@
     to_m[low_rows, :] = (mine_m + relay_m[...].astype(F32)).astype(BF16)
     sum_m.start()
     own_out = pltpu.make_async_copy(own_sum, o_ref, own_sem.at[0])
-    own_sum[top_rows, :] = project(top_rows, 0)
-    own_sum[low_rows, :] = project(low_rows, 0)
+    mine_top = project(top_rows, 0)
+    mine_low = project(low_rows, 0)
+    plain_m.wait_recv()
+    own_sum[top_rows, :] = mine_top + early_p[...].astype(F32)
+    plain_p.wait_recv()
+    own_sum[low_rows, :] = mine_low + early_m[...].astype(F32)
     own_out.start()
-    plain_p.wait_recv()
-    plain_m.wait_recv()
+    own_out.wait()
     sum_p.wait_recv()
     sum_m.wait_recv()
-    own_out.wait()
     for copy in (opp_p, opp_m, plain_p, plain_m, sum_p, sum_m):
         copy.wait_send()
     @pl.when(place < n_ctx - 1)
@@ -352,11 +370,11 @@
         parts = 1 + 2 * PIECES
         any_space = pl.BlockSpec(memory_space=pl.ANY)
         dma = pltpu.SemaphoreType.DMA
-        own, from_m, from_p = pl.pallas_call(
+        own, late = pl.pallas_call(
             functools.partial(kernel, hops, n_ctx, n_x),
-            out_shape=[jax.ShapeDtypeStruct((tokens, width), kind) for kind in (F32, BF16, BF16)],
+            out_shape=[jax.ShapeDtypeStruct((tokens, width), kind) for kind in (F32, BF16)],
             in_specs=[any_space] * 5,
-            out_specs=[any_space] * 3,
+            out_specs=[any_space] * 2,
             scratch_shapes=[
                 pltpu.VMEM((tokens, width), BF16),
                 pltpu.VMEM((tokens, HEAD_DIM), BF16),
@@ -374,6 +392,8 @@
                 pltpu.VMEM((tokens, width), BF16),
                 pltpu.VMEM((half, width), BF16),
                 pltpu.VMEM((half, width), BF16),
+                pltpu.VMEM((half, width), BF16),
+                pltpu.VMEM((half, width), BF16),
                 pltpu.VMEM((tokens, width), F32),
                 pltpu.VMEM((1, tokens), jnp.int32),
                 pltpu.VMEM((tokens, HEAD_DIM), BF16),
@@ -389,7 +409,7 @@
             ],
             compiler_params=pltpu.CompilerParams(collective_id=0, has_side_effects=True),
         )(queries, keys, values, segment_ids.reshape(1, tokens), out_weight)
-        return (own + from_m.astype(F32) + from_p.astype(F32)).astype(BF16)
+        return (own + late.astype(F32)).astype(BF16)
 
     in_specs = (P("ctx", "head"), P("ctx", "head"), P("ctx", "head"), P("ctx"), P("head", None))
     return jax.shard_map(body, mesh=mesh, in_specs=in_specs, out_specs=P("ctx", "head"), check_vma=False)

time: 57.2 us -> 57.1 us (level)
  the two profiles are of different devices: /device:TPU:48 before, /device:TPU:120 now
where the time goes in v4:
time: 57.1 us; the launch traced here: 57 us
  Pallas kernels  55.1 us (96%)
  other arithmetic  1.88 us (3%)
    pallas_call x1, Pallas kernels, body(): pl.pallas_call(functools.partial(kernel, hops, n_ctx, n_x), out_shape=[ja...  55.1 us
    convert_element_type x1, other arithmetic, body(): return (own + late.astype(F32)).astype(BF16)  1.88 us

profile of v4, /device:TPU:120, one launch (start us, length us, event | category | flops | bytes accessed | tf_op | source)
XLA Modules:
  0.0 57.0 jit_solution(13647280390793347531)
XLA Ops:
  0.0 55.1 %shard_map.55 = (f32[256,512]{1,0:T(8,128)}, bf16[256,512]{1,0:T(8,128)(2,1)}) custom-call(bf16[256,512]{1,0:T(8,128)(2,1)} %q_hbm.1, bf16[256,128]{1,0:T(8,128)(2,1)} %k_hbm.1, bf16[256,128]{1,0:T(8,128)(2,1)} %v_hbm.1, s32[1,256]{1,0:T(1,128)} %bitcast.1, bf16[512,4096]{1,0:T(8,128)(2,1)} %w_hbm.1), custom_call_target="tpu_custom_call" | custom-call | tf_op jit(solution)/shard_map/pallas_call | solution.py:373
  55.1 1.9 %add_convert_fusion = bf16[256,512]{1,0:T(8,128)(2,1)} fusion(f32[256,512]{1,0:T(8,128)} %get-tuple-element.7, bf16[256,512]{1,0:T(8,128)(2,1)} %get-tuple-element.8), kind=kLoop, calls=%fused_computation | loop fusion | flops 393216 | bytes 1048576 | tf_op jit(solution)/shard_map/convert_element_type | solution.py:412

commit v5 on v4

--- a/solution.py
+++ b/solution.py
@@ -11,7 +11,7 @@
 HEAD_DIM = 128
 DOC_MAX = 1792
 RING = 16
-PIECES = 4
+PIECES = 2
 MESH = pl.DeviceIdType.MESH
 NEG = -1e30
 F32 = jnp.float32

time: 57.1 us -> 57 us (level)
  no operation moved by 1% of the time
where the time goes in v5:
time: 57 us; the launch traced here: 56.9 us
  Pallas kernels  55 us (96%)
  other arithmetic  1.88 us (3%)
    pallas_call x1, Pallas kernels, body(): pl.pallas_call(functools.partial(kernel, hops, n_ctx, n_x), out_shape=[ja...  55 us
    convert_element_type x1, other arithmetic, body(): return (own + late.astype(F32)).astype(BF16)  1.88 us

profile of v5, /device:TPU:120, one launch (start us, length us, event | category | flops | bytes accessed | tf_op | source)
XLA Modules:
  0.0 56.9 jit_solution(2557440084861568324)
XLA Ops:
  0.0 55.0 %shard_map.55 = (f32[256,512]{1,0:T(8,128)}, bf16[256,512]{1,0:T(8,128)(2,1)}) custom-call(bf16[256,512]{1,0:T(8,128)(2,1)} %q_hbm.1, bf16[256,128]{1,0:T(8,128)(2,1)} %k_hbm.1, bf16[256,128]{1,0:T(8,128)(2,1)} %v_hbm.1, s32[1,256]{1,0:T(1,128)} %bitcast.1, bf16[512,4096]{1,0:T(8,128)(2,1)} %w_hbm.1), custom_call_target="tpu_custom_call" | custom-call | tf_op jit(solution)/shard_map/pallas_call | solution.py:373
  55.0 1.9 %add_convert_fusion = bf16[256,512]{1,0:T(8,128)(2,1)} fusion(f32[256,512]{1,0:T(8,128)} %get-tuple-element.7, bf16[256,512]{1,0:T(8,128)(2,1)} %get-tuple-element.8), kind=kLoop, calls=%fused_computation | loop fusion | flops 393216 | bytes 1048576 | tf_op jit(solution)/shard_map/convert_element_type | solution.py:412
